TPU v7x, 32 devices: a whole 2x2x4 slice. The times are simulated.
32 devices in a mesh: row: 16 (over z, x, core), col: 2 (over y).
Axes of the slice: x: 2, y: 2, z: 4, core: 2. Of those that a mesh axis runs over, the one named last changes fastest.
Arguments:
- features: bfloat16 [4096, 256], P(('row', 'col')), may hold values from -6 to 6
- weight: bfloat16 [256, 256], replicated, may hold values from -0.375 to 0.375
- grad_out: bfloat16 [4096, 256], P(('row', 'col')), may hold values from -6 to 6
- tiles: bfloat16 [16, 2, 24, 128, 128], P('row', 'col'), may hold values from -0.109375 to 0.109375
- slots: int32 [16, 2, 24], P('row', 'col'), may hold values from 0 to 31, as said below
Outputs:
- activated: bfloat16 [4096, 256], P(('row', 'col'))
- grad_weight: float32 [256, 256], replicated
- grad_in: bfloat16 [4096, 256], P(('row', 'col'))
Inputs may be any that keep to these rules, and one draw needn't show every extreme that they name: `slots`: within one tile the 24 entries are distinct.
All inputs are finite; a program needn't handle non-finite values.
Results may differ from a plain program's by a relative error of at most 0.0061.
Values may be sent and summed in bfloat16 or wider, within the bound.
No kernel may reach another device: no remote copies, remote signals or barrier semaphores. Data moves between devices by JAX's collectives and lax.ppermute only.
A program may use at most 128 MiB of HBM per device.

v0:
```python
import math
import jax
import jax.numpy as jnp
from jax import lax
from jax.sharding import PartitionSpec as P


def local(features, weight, grad_out, tiles, slots):
    tile_blocks = tiles[0, 0]
    tile_slots = slots[0, 0]
    own_rows, width = features.shape
    side = tile_blocks.shape[1]
    row_count = lax.axis_size("row")
    col_count = lax.axis_size("col")
    row_blocks = col_count * own_rows // side
    col_blocks = row_count * own_rows // side
    dense_tile = (
        jnp.zeros((row_blocks * col_blocks, side, side), jnp.bfloat16)
        .at[tile_slots]
        .set(tile_blocks)
    )
    dense_tile = dense_tile.reshape(row_blocks, col_blocks, side, side)
    column_panel = lax.all_gather(features, "row", axis=0, tiled=True).reshape(
        col_blocks, side, width
    )
    row_partial = jnp.einsum(
        "bcij,cjf->bif", dense_tile, column_panel, preferred_element_type=jnp.float32
    )
    row_partial = row_partial.reshape(row_blocks * side, width)
    aggregated = lax.psum_scatter(row_partial, "col", scatter_dimension=0, tiled=True).astype(
        jnp.bfloat16
    )
    pre = jnp.dot(aggregated, weight, preferred_element_type=jnp.float32)
    sigmoid_pre = jax.nn.sigmoid(pre)
    activated = (pre * sigmoid_pre).astype(jnp.bfloat16)
    grad_pre = (
        grad_out.astype(jnp.float32) * sigmoid_pre * (1.0 + pre * (1.0 - sigmoid_pre))
    ).astype(jnp.bfloat16)
    weight_term = jnp.dot(aggregated.T, grad_pre, preferred_element_type=jnp.float32)
    total_nodes = own_rows * row_count * col_count
    grad_weight = lax.psum(weight_term, ("row", "col")) * (1.0 / math.sqrt(total_nodes))
    grad_agg = jnp.dot(grad_pre, weight.T, preferred_element_type=jnp.float32).astype(jnp.bfloat16)
    row_panel = lax.all_gather(grad_agg, "col", axis=0, tiled=True).reshape(row_blocks, side, width)
    col_partial = jnp.einsum(
        "bcij,bif->cjf", dense_tile, row_panel, preferred_element_type=jnp.float32
    )
    col_partial = col_partial.reshape(col_blocks * side, width)
    summed = lax.psum_scatter(col_partial, "row", scatter_dimension=0, tiled=True)
    grad_in = summed.astype(jnp.bfloat16)
    return (activated, grad_weight, grad_in)


def solution(mesh):
    in_specs = (
        P(("row", "col"), None),
        P(),
        P(("row", "col"), None),
        P("row", "col", None, None, None),
        P("row", "col", None),
    )
    out_specs = (P(("row", "col"), None), P(), P(("row", "col"), None))
    return jax.shard_map(local, mesh=mesh, in_specs=in_specs, out_specs=out_specs, check_vma=False)
```

profile of v0, /device:TPU:0, one launch (start us, length us, event | category | flops | bytes accessed | tf_op | source)
XLA Modules:
  0.0 269.0 jit_solution(17586135211824430519)
XLA Ops:
  7.2 0.0 all-gather.2.cloned.1.call-start
  7.2 0.7 all-gather.2.cloned.1.call-update
  7.9 0.0 reduce-scatter.3.cloned.1.call-start
  8.0 0.7 fusion.4
  8.6 0.2 broadcast_in_dim.4
  8.9 3.5 %scatter_fusion = bf16[32,128,128]{2,1,0:T(8,128)(2,1)S(1)} fusion(bf16[32,128,128]{2,1,0:T(8,128)(2,1)S(1)} %broadcast_in_dim.4, s32[24]{0:T(128)S(1)} %fusion.4, bf16[24,128,128]{2,1,0:T(8,128)(2,1)} %bitcast.29), kind=kCustom, calls=%fused_computation | custom fusion | bytes 2359392 | tf_op jit(solution)/shard_map/scatter | solution.py:20
  12.4 0.1 copy.9
  12.5 38.4 %all-gather.2.cloned.1.call-done = bf16[2048,256]{1,0:T(8,128)(2,1)} async-done(((bf16[128,256]{1,0:T(8,128)(2,1)}), bf16[2048,256]{1,0:T(8,128)(2,1)}) %all-gather.2.cloned.1.call-update) | async-done | bytes 1048592 | tf_op jit(solution)/shard_map/all_gather | solution.py:23
  50.8 2.4 convolution_bitcast_fusion.1
  53.2 0.0 reduce-scatter.3.cloned.1.call-update
  53.2 0.0 all-reduce.2.cloned.1.call-start
  53.3 0.7 copy.10
  54.0 10.3 %reduce-scatter.3.cloned.1.call-done = f32[128,256]{1,0:T(8,128)} async-done(((f32[256,256]{1,0:T(8,128)}), f32[128,256]{1,0:T(8,128)}) %reduce-scatter.3.cloned.1.call-update) | async-done | bytes 131088 | tf_op jit(solution)/shard_map/reduce_scatter | solution.py:30
  64.3 1.7 multiply_convert_fusion.1
  66.0 0.2 convolution_convert_fusion
  66.2 1.8 fusion
  68.1 0.0 reduce-scatter.5.cloned.1.call-start
  68.1 4.9 %all_gather.7 = bf16[256,256]{1,0:T(8,128)(2,1)S(1)} all-gather(bf16[128,256]{1,0:T(8,128)(2,1)S(1)} %convolution_convert_fusion), channel_id=1, replica_groups=mesh['row'=16,'col'=2] {'col'}, dimensions={0}, use_global_device_ids=true | all-gather | bytes 196608 | tf_op jit(solution)/shard_map/all_gather | solution.py:43
  73.1 1.8 convolution_bitcast_fusion
  74.8 0.0 reduce-scatter.5.cloned.1.call-update
  74.9 121.4 %all-reduce.2.cloned.1.call-done = f32[256,256]{1,0:T(8,128)} async-done(((f32[256,256]{1,0:T(8,128)}), f32[256,256]{1,0:T(8,128)}) %all-reduce.2.cloned.1.call-update) | async-done | bytes 262160 | tf_op jit(solution)/shard_map/psum | solution.py:41
  196.3 1.7 broadcast_multiply_fusion
  197.9 63.0 %reduce-scatter.5.cloned.1.call-done = f32[128,256]{1,0:T(8,128)} async-done(((f32[2048,256]{1,0:T(8,128)}), f32[128,256]{1,0:T(8,128)}) %reduce-scatter.5.cloned.1.call-update) | async-done | bytes 131088 | tf_op jit(solution)/shard_map/reduce_scatter | solution.py:48
  260.9 1.5 convert_element_type.23
  (5 shorter events, 0.0 us)
Async XLA Ops:
  7.2 57.1 %copy-start = (bf16[256,256]{1,0:T(8,128)(2,1)S(1)}, bf16[256,256]{1,0:T(8,128)(2,1)}, u32[]{:S(2)}) copy-start(bf16[256,256]{1,0:T(8,128)(2,1)} %param.6) | copy-start | bytes 393220
  7.2 43.7 %all-gather.2.cloned.1.call-start = ((), (), s32[]{:S(2)}) async-start(), calls=%async_computation.2 | async-start | bytes 1114112 | tf_op jit(solution)/shard_map/all_gather | solution.py:23
  7.9 56.4 %reduce-scatter.3.cloned.1.call-start = ((), (), s32[]{:S(2)}) async-start(), calls=%async_computation.3 | async-start | bytes 393216 | tf_op jit(solution)/shard_map/reduce_scatter | solution.py:30
  53.2 12.8 %copy-start.1 = (bf16[128,256]{1,0:T(8,128)(2,1)S(1)}, bf16[128,256]{1,0:T(8,128)(2,1)}, u32[]{:S(2)}) copy-start(bf16[128,256]{1,0:T(8,128)(2,1)} %param.7) | copy-start | bytes 196612
  53.2 143.0 %all-reduce.2.cloned.1.call-start = ((), (), s32[]{:S(2)}) async-start(), calls=%async_computation.4 | async-start | bytes 524288 | tf_op jit(solution)/shard_map/psum | solution.py:41
  68.1 192.9 %reduce-scatter.5.cloned.1.call-start = ((), (), s32[]{:S(2)}) async-start(), calls=%async_computation.5 | async-start | bytes 2228224 | tf_op jit(solution)/shard_map/reduce_scatter | solution.py:48
Sparse Core Ops, SparseCore 0:
  10.2 40.6 all-gather.1
  53.6 10.5 reduce-scatter.2
  71.3 124.9 all-reduce.1
  200.3 60.5 reduce-scatter.4
where the time goes:
time: 269 us
  waiting for transfers between devices  234 us (87%)
  between operations  13.8 us (5%)
  matrix products  7.9 us (3%)
  blocking collectives  4.94 us (2%)
  local copies, waits for them, and re-layouts  4.5 us (2%)
  other arithmetic  3.87 us (1%)
    psum x1, waiting for transfers between devices, local(): lax.psum(weight_term, ('row', 'col')) * (1.0 / math.sqrt(total_nodes))  121 us
    reduce_scatter x1, waiting for transfers between devices, local(): lax.psum_scatter(col_partial, 'row', scatter_dimension=0, tiled=True)  63 us
    all_gather x1, waiting for transfers between devices, local(): lax.all_gather(features, 'row', axis=0, tiled=True)  38.4 us
    reduce_scatter x1, waiting for transfers between devices, local(): lax.psum_scatter(row_partial, 'col', scatter_dimension=0, tiled=True)  10.3 us
  transfers between devices with their start and end apart: 4, of which 4 were waited for; matrix products, arithmetic and copies ran while one was open for 3% of the time, Pallas kernels for 0%

commit v1 on v0

--- a/solution.py
+++ b/solution.py
@@ -38,7 +38,7 @@
     ).astype(jnp.bfloat16)
     weight_term = jnp.dot(aggregated.T, grad_pre, preferred_element_type=jnp.float32)
     total_nodes = own_rows * row_count * col_count
-    grad_weight = lax.psum(weight_term, ("row", "col")) * (1.0 / math.sqrt(total_nodes))
+    grad_weight = lax.psum(lax.psum(weight_term, "col"), "row") * (1.0 / math.sqrt(total_nodes))
     grad_agg = jnp.dot(grad_pre, weight.T, preferred_element_type=jnp.float32).astype(jnp.bfloat16)
     row_panel = lax.all_gather(grad_agg, "col", axis=0, tiled=True).reshape(row_blocks, side, width)
     col_partial = jnp.einsum(

time: 269 us -> 257 us (0.955)
  waiting for transfers between devices: 234 us -> 222 us
    psum x1 -> x2, waiting for transfers between devices: 121 us -> 108 us  [the longest x1 90.2 us: local(): lax.psum(lax.psum(weight_term, 'col'), 'row')]
  transfers between devices with their start and end apart: 4 -> 5, of which waited for: 4 -> 5; matrix products, arithmetic and copies ran while one was open for 3% -> 3% of each run, Pallas kernels for 0% -> 0%
where the time goes in v1:
time: 257 us
  waiting for transfers between devices  222 us (86%)
  between operations  13.8 us (5%)
  matrix products  7.89 us (3%)
  blocking collectives  4.94 us (2%)
  local copies, waits for them, and re-layouts  4.5 us (2%)
  other arithmetic  3.87 us (2%)
    psum x1, waiting for transfers between devices, local(): lax.psum(lax.psum(weight_term, 'col'), 'row')  90.2 us
    reduce_scatter x1, waiting for transfers between devices, local(): lax.psum_scatter(col_partial, 'row', scatter_dimension=0, tiled=True)  64 us
    all_gather x1, waiting for transfers between devices, local(): lax.all_gather(features, 'row', axis=0, tiled=True)  38.4 us
    psum x1, waiting for transfers between devices, local(): lax.psum(weight_term, 'col')  18.2 us
    reduce_scatter x1, waiting for transfers between devices, local(): lax.psum_scatter(row_partial, 'col', scatter_dimension=0, tiled=True)  10.3 us
  transfers between devices with their start and end apart: 5, of which 5 were waited for; matrix products, arithmetic and copies ran while one was open for 3% of the time, Pallas kernels for 0%

profile of v1, /device:TPU:0, one launch (start us, length us, event | category | flops | bytes accessed | tf_op | source)
XLA Modules:
  0.0 257.0 jit_solution(1827048118813412140)
XLA Ops:
  7.2 0.0 all-gather.2.cloned.1.call-start
  7.2 0.7 all-gather.2.cloned.1.call-update
  7.9 0.0 reduce-scatter.3.cloned.1.call-start
  8.0 0.7 fusion.4
  8.6 0.2 broadcast_in_dim.4
  8.9 3.5 %scatter_fusion = bf16[32,128,128]{2,1,0:T(8,128)(2,1)S(1)} fusion(bf16[32,128,128]{2,1,0:T(8,128)(2,1)S(1)} %broadcast_in_dim.4, s32[24]{0:T(128)S(1)} %fusion.4, bf16[24,128,128]{2,1,0:T(8,128)(2,1)} %bitcast.29), kind=kCustom, calls=%fused_computation | custom fusion | bytes 2359392 | tf_op jit(solution)/shard_map/scatter | solution.py:20
  12.4 0.1 copy.9
  12.5 38.4 %all-gather.2.cloned.1.call-done = bf16[2048,256]{1,0:T(8,128)(2,1)} async-done(((bf16[128,256]{1,0:T(8,128)(2,1)}), bf16[2048,256]{1,0:T(8,128)(2,1)}) %all-gather.2.cloned.1.call-update) | async-done | bytes 1048592 | tf_op jit(solution)/shard_map/all_gather | solution.py:23
  50.8 2.4 convolution_bitcast_fusion.1
  53.2 0.0 all-reduce.3.cloned.1.call-start
  53.3 0.7 copy.10
  54.0 10.3 %reduce-scatter.3.cloned.1.call-done = f32[128,256]{1,0:T(8,128)} async-done(((f32[256,256]{1,0:T(8,128)}), f32[128,256]{1,0:T(8,128)}) %reduce-scatter.3.cloned.1.call-update) | async-done | bytes 131088 | tf_op jit(solution)/shard_map/reduce_scatter | solution.py:30
  64.3 1.7 multiply_convert_fusion.1
  66.0 1.8 fusion
  67.9 0.0 all-reduce.5.cloned.1.call-start
  67.9 0.2 convolution_convert_fusion
  68.1 4.9 %all_gather.7 = bf16[256,256]{1,0:T(8,128)(2,1)S(1)} all-gather(bf16[128,256]{1,0:T(8,128)(2,1)S(1)} %convolution_convert_fusion), channel_id=1, replica_groups=mesh['row'=16,'col'=2] {'col'}, dimensions={0}, use_global_device_ids=true | all-gather | bytes 196608 | tf_op jit(solution)/shard_map/all_gather | solution.py:43
  73.1 18.2 %all-reduce.3.cloned.1.call-done = f32[256,256]{1,0:T(8,128)} async-done(((f32[256,256]{1,0:T(8,128)}), f32[256,256]{1,0:T(8,128)}) %all-reduce.3.cloned.1.call-update) | async-done | bytes 262160 | tf_op jit(solution)/shard_map/psum | solution.py:41
  91.2 0.0 reduce-scatter.5.cloned.1.call-start
  91.3 1.8 convolution_bitcast_fusion
  93.1 90.2 %all-reduce.5.cloned.1.call-done = f32[256,256]{1,0:T(8,128)} async-done(((f32[256,256]{1,0:T(8,128)}), f32[256,256]{1,0:T(8,128)}) %all-reduce.5.cloned.1.call-update) | async-done | bytes 262160 | tf_op jit(solution)/shard_map/psum | solution.py:41
  183.2 1.7 broadcast_multiply_fusion
  184.9 64.0 %reduce-scatter.5.cloned.1.call-done = f32[128,256]{1,0:T(8,128)} async-done(((f32[2048,256]{1,0:T(8,128)}), f32[128,256]{1,0:T(8,128)}) %reduce-scatter.5.cloned.1.call-update) | async-done | bytes 131088 | tf_op jit(solution)/shard_map/reduce_scatter | solution.py:48
  248.9 1.5 convert_element_type.23
  (8 shorter events, 0.1 us)
Async XLA Ops:
  7.2 57.1 %copy-start = (bf16[256,256]{1,0:T(8,128)(2,1)S(1)}, bf16[256,256]{1,0:T(8,128)(2,1)}, u32[]{:S(2)}) copy-start(bf16[256,256]{1,0:T(8,128)(2,1)} %param.6) | copy-start | bytes 393220
  7.2 43.7 %all-gather.2.cloned.1.call-start = ((), (), s32[]{:S(2)}) async-start(), calls=%async_computation.2 | async-start | bytes 1114112 | tf_op jit(solution)/shard_map/all_gather | solution.py:23
  7.9 56.4 %reduce-scatter.3.cloned.1.call-start = ((), (), s32[]{:S(2)}) async-start(), calls=%async_computation.3 | async-start | bytes 393216 | tf_op jit(solution)/shard_map/reduce_scatter | solution.py:30
  53.2 12.8 %copy-start.1 = (bf16[128,256]{1,0:T(8,128)(2,1)S(1)}, bf16[128,256]{1,0:T(8,128)(2,1)}, u32[]{:S(2)}) copy-start(bf16[128,256]{1,0:T(8,128)(2,1)} %param.7) | copy-start | bytes 196612
  53.2 38.0 %all-reduce.3.cloned.1.call-start = ((), (), s32[]{:S(2)}) async-start(), calls=%async_computation.4 | async-start | bytes 524288 | tf_op jit(solution)/shard_map/psum | solution.py:41
  67.9 115.4 %all-reduce.5.cloned.1.call-start = ((), (), s32[]{:S(2)}) async-start(), calls=%async_computation.5 | async-start | bytes 524288 | tf_op jit(solution)/shard_map/psum | solution.py:41
  91.2 157.7 %reduce-scatter.5.cloned.1.call-start = ((), (), s32[]{:S(2)}) async-start(), calls=%async_computation.6 | async-start | bytes 2228224 | tf_op jit(solution)/shard_map/reduce_scatter | solution.py:48
Sparse Core Ops, SparseCore 0:
  10.2 40.6 all-gather.1
  53.6 10.5 reduce-scatter.2
  68.0 23.1 all-reduce.2
  94.5 88.7 all-reduce.4
  186.8 62.0 reduce-scatter.4
